TPU v7x, 32 devices: a whole 2x2x4 slice. The times are simulated.
32 devices in a mesh: groups: 1, expert: 8 (over z, y), tensor: 2 (over x), pair: 2 (over core).
Axes of the slice: x: 2, y: 2, z: 4, core: 2. Of those that a mesh axis runs over, the one named last changes fastest.
Arguments:
- tokens: bfloat16 [512, 3584], P(('groups', 'expert', 'tensor', 'pair')), may hold values from -6 to 6
- expert_ids: int32 [512, 8], P(('groups', 'expert', 'tensor', 'pair')), may hold values from 0 to 15, all different within a row; in each aligned block of 16 rows (0 to 15, 16 to 31, ...) at most 16 rows name the same one
- route_weight: float32 [512, 8], P(('groups', 'expert', 'tensor', 'pair')), may hold values from 0.05 to 0.5
- w_gate: bfloat16 [16, 3584, 1024], P(('expert', 'pair'), None, 'tensor'), may hold values from -0.09375 to 0.09375
- w_up: bfloat16 [16, 3584, 1024], P(('expert', 'pair'), None, 'tensor'), may hold values from -0.09375 to 0.09375
- w_down: bfloat16 [16, 1024, 3584], P(('expert', 'pair'), 'tensor'), may hold values from -0.1875 to 0.1875
- s_gate: bfloat16 [3584, 2048], P(None, ('tensor', 'pair')), may hold values from -0.09375 to 0.09375
- s_up: bfloat16 [3584, 2048], P(None, ('tensor', 'pair')), may hold values from -0.09375 to 0.09375
- s_down: bfloat16 [2048, 3584], P(('tensor', 'pair')), may hold values from -0.125 to 0.125
Outputs:
- moe_out: bfloat16 [512, 3584], P(('groups', 'expert', 'tensor', 'pair'))
Inputs may be any that keep to these rules, and one draw needn't show every extreme that they name: `expert_ids`: each row names 8 different experts. Among the 16 tokens of one device no expert is named by more than 16 tokens, and in every draw some expert is named by exactly 16 tokens of some device.
All inputs are finite; a program needn't handle non-finite values.
Results may differ from a plain program's by a relative error of at most 0.014.
Values may be sent and summed in bfloat16 or wider, within the bound.
A program may use at most 64 MiB of HBM per device.

v0:
```python
import jax
import jax.numpy as jnp
from jax import lax
from jax.sharding import PartitionSpec as P


def per_device(tokens, expert_ids, route_weight, w_gate, w_up, w_down, s_gate, s_up, s_down):
    tok_rows, model_width = tokens.shape
    top_count = expert_ids.shape[1]
    owners = lax.axis_size(("expert", "pair"))
    row_piece = lax.all_gather(tokens, ("tensor", "pair"), axis=0, tiled=True)
    gate_part = jnp.dot(row_piece, s_gate, preferred_element_type=jnp.float32)
    upper_part = jnp.dot(row_piece, s_up, preferred_element_type=jnp.float32)
    shared_act = (jax.nn.silu(gate_part) * upper_part).astype(jnp.bfloat16)
    shared = lax.psum_scatter(
        jnp.dot(shared_act, s_down, preferred_element_type=jnp.float32).astype(jnp.bfloat16),
        ("tensor", "pair"),
        scatter_dimension=0,
        tiled=True,
    ).astype(jnp.float32)
    labels = jnp.arange(owners, dtype=jnp.int32)
    matches = expert_ids[:, :, None] == labels[None, None, :]
    chosen = jnp.any(matches, axis=1)
    weight = jnp.sum(jnp.where(matches, route_weight[:, :, None], 0.0), axis=1)
    slot_total = min(tok_rows, 2 * tok_rows * top_count // owners)
    position = jnp.cumsum(chosen.astype(jnp.int32), axis=0) - 1
    placement = chosen[:, :, None] & (
        position[:, :, None] == jnp.arange(slot_total, dtype=jnp.int32)[None, None, :]
    )
    outgoing = jnp.einsum(
        "tec,td->ecd", placement.astype(jnp.bfloat16), tokens, preferred_element_type=jnp.float32
    ).astype(jnp.bfloat16)
    n_expert = lax.axis_size("expert")
    n_tensor = lax.axis_size("tensor")
    n_pair = lax.axis_size("pair")
    copies = jnp.broadcast_to(
        outgoing.reshape(n_expert, 1, n_pair, slot_total, model_width),
        (n_expert, n_tensor, n_pair, slot_total, model_width),
    )
    copies = copies.reshape(n_expert * n_tensor * n_pair, slot_total, model_width)
    arrived = lax.all_to_all(
        copies, ("expert", "tensor", "pair"), split_axis=0, concat_axis=0, tiled=True
    )
    senders, slot_count, _ = arrived.shape
    flattened = arrived.reshape(senders * slot_count, model_width)
    gate_part = jnp.dot(flattened, w_gate[0], preferred_element_type=jnp.float32)
    upper_part = jnp.dot(flattened, w_up[0], preferred_element_type=jnp.float32)
    hidden = (jax.nn.silu(gate_part) * upper_part).astype(jnp.bfloat16)
    partial_value = jnp.dot(hidden, w_down[0], preferred_element_type=jnp.float32).astype(
        jnp.bfloat16
    )
    partial_value = partial_value.reshape(senders, slot_count, model_width)
    returning = lax.all_to_all(
        partial_value, ("expert", "tensor", "pair"), split_axis=0, concat_axis=0, tiled=True
    )
    grouped = returning.reshape(n_expert, n_tensor, n_pair, slot_count, model_width).astype(
        jnp.float32
    )
    summed = jnp.sum(grouped, axis=1).reshape(n_expert * n_pair, slot_count, model_width)
    returned = summed.astype(jnp.bfloat16)
    combine_scale = (placement.astype(jnp.float32) * weight[:, :, None]).reshape(
        tok_rows, owners * slot_total
    )
    routed = jnp.dot(
        combine_scale,
        returned.reshape(owners * slot_total, model_width).astype(jnp.float32),
        precision=lax.Precision.HIGHEST,
    )
    return (shared + routed).astype(jnp.bfloat16)


def solution(mesh):
    in_specs = (
        P(("groups", "expert", "tensor", "pair"), None),
        P(("groups", "expert", "tensor", "pair"), None),
        P(("groups", "expert", "tensor", "pair"), None),
        P(("expert", "pair"), None, "tensor"),
        P(("expert", "pair"), None, "tensor"),
        P(("expert", "pair"), "tensor", None),
        P(None, ("tensor", "pair")),
        P(None, ("tensor", "pair")),
        P(("tensor", "pair"), None),
    )
    out_specs = P(("groups", "expert", "tensor", "pair"), None)
    return jax.shard_map(
        per_device, mesh=mesh, in_specs=in_specs, out_specs=out_specs, check_vma=False
    )
```

profile of v0, /device:TPU:0, one launch (start us, length us, event | category | flops | bytes accessed | tf_op | source)
XLA Modules:
  0.0 213.8 jit_solution(6730240935387070470)
XLA Ops:
  6.5 0.8 copy.15
  7.3 0.1 fusion.31
  7.4 0.1 copy.16
  7.5 0.1 copy.17
  7.6 1.8 convolution_convert_fusion.1
  9.4 0.4 broadcast_in_dim.29
  9.9 90.2 %all_to_all.10 = bf16[32,16,3584]{2,1,0:T(8,128)(2,1)S(1)} all-to-all(bf16[32,16,3584]{2,1,0:T(8,128)(2,1)S(1)} %bitcast.38), channel_id=1, replica_groups=mesh['groups'=1,'expert'=8,'tensor'=2,'pair'=2] {'expert','tensor','pair'}, dimensions={0} | all-to-all | bytes 7340032 | tf_op jit(solution)/shard_map/all_to_all | solution.py:41
  100.0 1.8 copy-done
  101.9 2.0 fusion.5
  103.9 10.0 %convolution_convert_fusion = bf16[512,3584]{1,0:T(8,128)(2,1)} fusion(bf16[1,512,3584]{2,1,0:T(8,128)(2,1)} %param.14, bf16[512,3584]{1,0:T(8,128)(2,1)} %bitcast.43, bf16[1,3584,512]{2,1,0:T(8,128)(2,1)} %param.13, f32[512,512]{1,0:T(8,128)S(1)} %fusion.5), kind=kOutput, calls=%fused_computation | convolution fusion | flops 3761504256 | bytes 15728640 | tf_op jit(solution)/shard_map/dot_general | solution.py:49
  114.0 3.7 %all-to-all-start.1 = ((bf16[32,16,3584]{2,1,0:T(8,128)(2,1)}), bf16[32,16,3584]{2,1,0:T(8,128)(2,1)}, u32[]{:S(2)}, u32[]{:S(2)}) async-start(bf16[32,16,3584]{2,1,0:T(8,128)(2,1)} %bitcast.41), calls=%async_computation.2 | async-start | bytes 7340032 | tf_op jit(solution)/shard_map/all_to_all | solution.py:53
  117.6 0.0 reduce-scatter.2.cloned.1.call-start
  117.7 28.8 %all_gather.3 = bf16[64,3584]{1,0:T(8,128)(2,1)S(1)} all-gather(bf16[16,3584]{1,0:T(8,128)(2,1)S(1)} %copy-done.1), channel_id=1, replica_groups=mesh['groups'=1,'expert'=8,'tensor'=2,'pair'=2] {'tensor','pair'}, dimensions={0}, use_global_device_ids=true | all-gather | bytes 573440 | tf_op jit(solution)/shard_map/all_gather | solution.py:11
  146.5 2.8 %fusion.38 = f32[64,512]{1,0:T(8,128)S(1)} fusion(bf16[64,3584]{1,0:T(8,128)(2,1)S(1)} %all_gather.3, bf16[3584,512]{1,0:T(8,128)(2,1)} %param.15), kind=kOutput, calls=%fused_computation.39 | convolution fusion | flops 234881024 | bytes 4259840 | tf_op jit(solution)/shard_map/dot_general | solution.py:12
  149.3 0.0 copy-start.2
  149.3 5.4 %convolution_convert_fusion.2 = bf16[64,3584]{1,0:T(8,128)(2,1)} fusion(bf16[512,3584]{1,0:T(8,128)(2,1)} %param.17, bf16[64,3584]{1,0:T(8,128)(2,1)S(1)} %all_gather.3, bf16[3584,512]{1,0:T(8,128)(2,1)} %param.16, f32[64,512]{1,0:T(8,128)S(1)} %fusion.38), kind=kOutput, calls=%fused_computation.2 | convolution fusion | flops 470188032 | bytes 8388608 | tf_op jit(solution)/shard_map/dot_general | solution.py:16
  154.7 0.0 reduce-scatter.2.cloned.1.call-update
  154.7 0.1 copy.18
  154.8 0.1 select_reduce_fusion
  154.9 0.1 copy.19
  155.0 45.4 %all-to-all-done.1 = bf16[32,16,3584]{2,1,0:T(8,128)(2,1)} async-done(((bf16[32,16,3584]{2,1,0:T(8,128)(2,1)}), bf16[32,16,3584]{2,1,0:T(8,128)(2,1)}, u32[]{:S(2)}, u32[]{:S(2)}) %all-to-all-start.1) | async-done | bytes 3670048 | tf_op jit(solution)/shard_map/all_to_all | solution.py:53
  200.4 2.9 %reduce = bf16[8,2,16,3584]{3,2,1,0:T(8,128)(2,1)S(1)} reduce(bf16[8,2,2,16,3584]{4,3,2,1,0:T(8,128)(2,1)} %bitcast.8, bf16[]{:T(256)} %constant.23), dimensions={1}, to_apply=%region_4.5.clone | reduce | flops 917504 | bytes 5505026 | tf_op jit(solution)/shard_map/reduce_sum | solution.py:59
  203.3 0.0 reduce-scatter.2.cloned.1.call-done
  203.3 3.6 %fusion.1 = bf16[16,3584]{1,0:T(8,128)(2,1)} fusion(bf16[16,16,3584]{2,1,0:T(8,128)(2,1)S(1)} %bitcast.39, bf16[16,3584]{1,0:T(8,128)(2,1)} %reduce-scatter.2.cloned.1.call-done, f32[16,16]{0,1:T(8,128)S(1)} %copy.19, s32[16,16]{0,1:T(8,128)S(1)} %copy.17, pred[16,16]{0,1:T(8,128)(4,1)S(1)} %copy.16), kind=kOutput, calls=%fused_computation.5 | convolution fusion | flops 176345088 | bytes 2066688 | tf_op jit(solution)/shard_map/dot_general | solution.py:64
  (9 shorter events, 0.1 us)
Async XLA Ops:
  9.9 92.0 %copy-start.3 = (bf16[1,3584,512]{2,1,0:T(8,128)(2,1)S(1)}, bf16[1,3584,512]{2,1,0:T(8,128)(2,1)}, u32[]{:S(2)}) copy-start(bf16[1,3584,512]{2,1,0:T(8,128)(2,1)} %param.12) | copy-start | bytes 11010052
  100.0 1.8 copy-start
  114.0 3.7 %copy-start.1 = (bf16[16,3584]{1,0:T(8,128)(2,1)S(1)}, bf16[16,3584]{1,0:T(8,128)(2,1)}, u32[]{:S(2)}) copy-start(bf16[16,3584]{1,0:T(8,128)(2,1)} %param.9) | copy-start | bytes 344068
  114.0 86.4 %all-to-all-start.1 = ((bf16[32,16,3584]{2,1,0:T(8,128)(2,1)}), bf16[32,16,3584]{2,1,0:T(8,128)(2,1)}, u32[]{:S(2)}, u32[]{:S(2)}) async-start(bf16[32,16,3584]{2,1,0:T(8,128)(2,1)} %bitcast.41), calls=%async_computation.2 | async-start | bytes 7340032 | tf_op jit(solution)/shard_map/all_to_all | solution.py:53
  117.6 85.7 %reduce-scatter.2.cloned.1.call-start = ((), (), s32[]{:S(2)}) async-start(), calls=%async_computation.3 | async-start | bytes 573440 | tf_op jit(solution)/shard_map/reduce_scatter | solution.py:15
  149.3 5.4 %copy-start.2 = (f32[16,8]{0,1:T(8,128)S(1)}, f32[16,8]{0,1:T(8,128)}, u32[]{:S(2)}) copy-start(f32[16,8]{0,1:T(8,128)} %param.11) | copy-start | bytes 1540
Sparse Core Ops, SparseCore 0:
  154.8 26.4 reduce-scatter.1
where the time goes:
time: 214 us
  blocking collectives  119 us (56%)
  waiting for transfers between devices  45.4 us (21%)
  matrix products  25.7 us (12%)
  between operations  13.5 us (6%)
  starting transfers between devices  3.71 us (2%)
  local copies, waits for them, and re-layouts  3.32 us (2%)
  other arithmetic  3.18 us (1%)
    all_to_all x1, blocking collectives, per_device(): lax.all_to_all(copies, ('expert', 'tensor', 'pair'), split_axis=0, concat...  90.2 us
    all_to_all x1, waiting for transfers between devices, per_device(): lax.all_to_all(partial_value, ('expert', 'tensor', 'pair'), split_axis=0,...  45.4 us
    all_gather x1, blocking collectives, per_device(): row_piece = lax.all_gather(tokens, ('tensor', 'pair'), axis=0, tiled=True)  28.8 us
    dot_general x1, matrix products, per_device(): jnp.dot(hidden, w_down[0], preferred_element_type=jnp.float32)  10 us
    dot_general x1, matrix products, per_device(): jnp.dot(shared_act, s_down, preferred_element_type=jnp.float32)  5.38 us
  transfers between devices with their start and end apart: 2, of which 1 were waited for; matrix products, arithmetic and copies ran while one was open for 5% of the time, Pallas kernels for 0%

commit v1 on v0

v1 whole, which is shorter than its diff:
```python
import functools

import jax
import jax.numpy as jnp
from jax import lax
from jax.experimental import pallas as pl
from jax.experimental.pallas import tpu as pltpu
from jax.sharding import PartitionSpec as P

MESH = pl.DeviceIdType.MESH
F32 = jnp.float32
BF16 = jnp.bfloat16


def lanes_for(experts):
    return -(-3 * experts // 128) * 128


def tile_of(width, most):
    for tile in range(min(width, most), 0, -1):
        if width % tile == 0 and (tile % 128 == 0 or tile == width):
            return tile
    return width


class Layout:
    def __init__(self, n_expert, n_tensor, n_pair, tok_rows):
        self.n_expert, self.n_tensor, self.n_pair = n_expert, n_tensor, n_pair
        self.ny = 2 if n_expert % 2 == 0 else 1
        self.nz = n_expert // self.ny
        self.swap = 1 if n_tensor == self.ny else 0
        self.na, self.nb = n_tensor, self.ny
        self.half = self.nz * self.na * self.nb
        self.blocks = 2 * self.half
        self.rows = tok_rows


def kernel(lay, experts, tok_in, ids, rw, wg_in, wu_in, wd_in, sg_in, su_in, sd_in, out,
           tok, part, recvp, recvb, recvl, recvr, recva, xs, hid, hs,
           wg, wu, wd, sg, su, sd, load_sem, tok_send, tok_recv, red_send, red_recv):
    nz, na, nb = lay.nz, lay.na, lay.nb
    rows, half = lay.rows, lay.half
    width = part.shape[-1]
    e_idx, t, p = lax.axis_index("expert"), lax.axis_index("tensor"), lax.axis_index("pair")
    z, y = e_idx // lay.ny, e_idx % lay.ny
    s = p * lay.swap
    a = t * (1 - s) + y * s
    b = y * (1 - s) + t * s

    def device(z_, b_, a_):
        t_ = a_ * (1 - s) + b_ * s
        y_ = b_ * (1 - s) + a_ * s
        return {"expert": z_ * lay.ny + y_, "tensor": t_, "pair": p}

    partner = {"expert": e_idx, "tensor": t, "pair": 1 - p}
    a_peers = [(a + d) % na for d in range(1, na)]
    b_peers = [(b + d) % nb for d in range(1, nb)]

    def place(q, z_, b_, a_):
        return ((q * nz + z_) * nb + b_) * na + a_

    own = place(p, z, b, a)
    first = pltpu.make_async_copy(tok_in, tok.at[own, :, pl.ds(0, width)], load_sem.at[6])
    first.start()
    loads = [
        pltpu.make_async_copy(src, dst, load_sem.at[i])
        for i, (src, dst) in enumerate(
            ((sg_in, sg), (su_in, su), (sd_in, sd), (wg_in.at[0], wg), (wu_in.at[0], wu), (wd_in.at[0], wd))
        )
    ]
    for load in loads:
        load.start()

    barrier = pltpu.get_barrier_semaphore()

    def greet(dev):
        pl.semaphore_signal(barrier, inc=1, device_id=dev, device_id_type=MESH)

    greet(partner)
    for a_ in a_peers:
        greet(device(z, b, a_))
    for b_ in b_peers:
        greet(device(z, b_, a))
    up, down = z < nz - 1, z > 0

    @pl.when(up)
    def _():
        greet(device(z + 1, b, a))

    @pl.when(down)
    def _():
        greet(device(z - 1, b, a))

    lane = lax.broadcasted_iota(jnp.int32, (rows, tok.shape[-1] - width), 1)
    top = ids.shape[1]
    pieces = [jnp.zeros(lane.shape, F32) for _ in range(3)]
    for k in range(top):
        for m in range(3):
            pieces[m] = pieces[m] + jnp.where(lane == ids[:, k : k + 1] + m * experts, rw[:, k : k + 1], 0.0)
    hi = [v.astype(BF16).astype(F32) for v in pieces]
    rest = [v - h for v, h in zip(pieces, hi)]
    mid = [v.astype(BF16).astype(F32) for v in rest]
    low = [v - h for v, h in zip(rest, mid)]
    tok[own, :, pl.ds(width, lane.shape[1])] = (hi[0] + mid[1] + low[2]).astype(BF16)

    line_peers = jnp.minimum(z, 1) + jnp.minimum(nz - 1 - z, 1)
    pl.semaphore_wait(barrier, na + nb - 1 + line_peers)

    first.wait()

    sent = []

    def both(c1, c2):
        return c2 if c1 is None else (c1 if c2 is None else jnp.logical_and(c1, c2))

    def run(cond, fn):
        if cond is None:
            fn()
        else:
            pl.when(cond)(fn)

    def send(src, dst, sem_send, sem_recv, dev, cond=None):
        copy = pltpu.make_async_remote_copy(
            src_ref=src, dst_ref=dst, send_sem=sem_send, recv_sem=sem_recv,
            device_id=dev, device_id_type=MESH)
        run(cond, copy.start)
        sent.append((cond, copy))

    counter = [0]

    def send_block(idx, dev, cond=None):
        send(tok.at[idx], tok.at[idx], tok_send.at[counter[0]], tok_recv.at[idx], dev, cond)
        counter[0] += 1

    def arrive(idx, cond=None):
        copy = pltpu.make_async_remote_copy(
            src_ref=tok.at[idx], dst_ref=tok.at[idx], send_sem=tok_send.at[0],
            recv_sem=tok_recv.at[idx], device_id=partner, device_id_type=MESH)
        run(cond, copy.wait_recv)

    for a_ in a_peers:
        send_block(own, device(z, b, a_))
    for k in range(nz):
        for step, a_ in enumerate([a] + a_peers):
            for sign in ((1, -1) if k else (0,)):
                z_ = z + sign * k
                cond = None if sign == 0 else (z_ < nz if sign > 0 else z_ >= 0)
                blk = place(p, z_, b, a_)
                if k or step:
                    arrive(blk, cond)
                if sign <= 0:
                    send_block(blk, device(z + 1, b, a), both(cond, up))
                if sign >= 0:
                    send_block(blk, device(z - 1, b, a), both(cond, down))
                for b_ in b_peers:
                    send_block(blk, device(z, b_, a), cond)
                send_block(blk, partner, cond)
    for k in range(nz):
        for b_ in b_peers:
            for a_ in [a] + a_peers:
                for sign in ((1, -1) if k else (0,)):
                    z_ = z + sign * k
                    cond = None if sign == 0 else (z_ < nz if sign > 0 else z_ >= 0)
                    blk = place(p, z_, b_, a_)
                    arrive(blk, cond)
                    send_block(blk, partner, cond)
    for z_ in range(nz):
        for b_ in range(nb):
            for a_ in range(na):
                arrive(place(1 - p, z_, b_, a_))

    group = []
    for q in range(2):
        for t_ in range(lay.n_tensor):
            sq = q * lay.swap
            group.append(place(q, z, t_ if sq else y, y if sq else t_))
    for i, idx in enumerate(group):
        xs[i] = tok[idx, :, pl.ds(0, width)]
    count = len(group)

    def hidden_tiles(x, w1, w2, scale, store):
        tile = tile_of(w1.shape[1], 256)

        def body(n, _):
            cols = pl.ds(pl.multiple_of(n * tile, tile), tile)
            g = jnp.dot(x(), w1[:, cols], preferred_element_type=F32)
            u = jnp.dot(x(), w2[:, cols], preferred_element_type=F32)
            h = g / (1.0 + jnp.exp(-g)) * u
            if scale is not None:
                h = h * scale
            store[:, cols] = h.astype(BF16)
            return 0

        lax.fori_loop(0, w1.shape[1] // tile, body, 0)

    loads[0].wait()
    loads[1].wait()
    hidden_tiles(lambda: xs[...].reshape(count * rows, width), sg, su, None, hs)
    loads[2].wait()
    for i in range(3, 6):
        loads[i].wait()

    out_tile = tile_of(width, 512)
    per = min(half, max(1, 256 // rows))
    while half % per:
        per -= 1
    mine = e_idx * lay.n_pair + p

    def chunk(c, _):
        at = c * per
        extra = tok[pl.ds(at, per), :, pl.ds(width, lane.shape[1])].reshape(per * rows, lane.shape[1])
        l2 = lax.broadcasted_iota(jnp.int32, extra.shape, 1)
        pick = (l2 == mine) | (l2 == mine + experts) | (l2 == mine + 2 * experts)
        scale = jnp.sum(jnp.where(pick, extra.astype(F32), 0.0), axis=1, keepdims=True)
        hidden_tiles(lambda: tok[pl.ds(at, per), :, pl.ds(0, width)].reshape(per * rows, width), wg, wu, scale, hid)

        def body(n, _):
            cols = pl.ds(pl.multiple_of(n * out_tile, out_tile), out_tile)
            v = jnp.dot(hid[...], wd[:, cols], preferred_element_type=F32)
            part[pl.ds(at, per), :, cols] = v.astype(BF16).reshape(per, rows, out_tile)
            return 0

        lax.fori_loop(0, width // out_tile, body, 0)
        return 0

    def shared_into(q):
        lo = q * (count // 2)

        def body(n, _):
            cols = pl.ds(pl.multiple_of(n * out_tile, out_tile), out_tile)
            r0 = pl.multiple_of(lo * rows, rows)
            v = jnp.dot(hs[pl.ds(r0, count // 2 * rows), :], sd[:, cols], preferred_element_type=F32)
            for j in range(count // 2):
                sq = q * lay.swap
                idx = place(q, z, j * sq + y * (1 - sq), y * sq + j * (1 - sq))
                part[idx, :, cols] = (part[idx, :, cols].astype(F32) + v[j * rows : (j + 1) * rows]).astype(BF16)
            return 0

        lax.fori_loop(0, width // out_tile, body, 0)

    rcount = [0]

    def send_sum(src, dst, recv_at, dev, cond=None):
        send(src, dst, red_send.at[rcount[0]], red_recv.at[recv_at], dev, cond)
        rcount[0] += 1

    def got(dst, recv_at, cond=None):
        copy = pltpu.make_async_remote_copy(
            src_ref=dst, dst_ref=dst, send_sem=red_send.at[0], recv_sem=red_recv.at[recv_at],
            device_id=partner, device_id_type=MESH)
        run(cond, copy.wait_recv)

    steps = half // per
    other = 1 - p
    lax.fori_loop(0, steps, lambda c, v: chunk(other * steps + c, v), 0)
    shared_into(other)

    def line_order():
        order = []
        for k in range(nz - 1, 0, -1):
            order += [(z + k, z + k < nz, 1), (z - k, z - k >= 0, -1)]
        return order + [(z, None, 0)]

    def p_slot(z_, b_):
        return z_ * nb + b_

    base_b = nz * nb
    base_l = base_b + (nb - 1) * nz
    base_r = base_l + nz
    base_a = base_r + nz

    def piece(q, z_, b_):
        return part.at[pl.ds(place(q, z_, b_, 0), na)]

    for b_ in list(range(nb)):
        for z_ in range(nz):
            slot = p_slot(z_, b_)
            send_sum(piece(other, z_, b_), recvp.at[slot], slot, partner)
    lax.fori_loop(0, steps, lambda c, v: chunk(p * steps + c, v), 0)
    shared_into(p)

    def add_into(q, z_, b_, others, cond):
        def fn():
            def blk(i, _):
                idx = place(q, z_, b_, i)
                v = part[idx].astype(F32)
                for ref in others:
                    v = v + ref[i].astype(F32)
                part[idx] = v.astype(BF16)
                return 0
            lax.fori_loop(0, na, blk, 0)
        run(cond, fn)

    for z_, cond, sign in line_order():
        for d, b_ in enumerate(b_peers):
            got(recvp.at[p_slot(z_, b_)], p_slot(z_, b_), cond)
            add_into(p, z_, b_, [recvp.at[p_slot(z_, b_)]], cond)
            send_sum(piece(p, z_, b_), recvb.at[d * nz + z_], base_b + d * nz + z_, device(z, b_, a), cond)
    for z_, cond, sign in line_order():
        got(recvp.at[p_slot(z_, b)], p_slot(z_, b), cond)
        others = [recvp.at[p_slot(z_, b)]]
        for d in range(nb - 1):
            got(recvb.at[d * nz + z_], base_b + d * nz + z_, cond)
            others.append(recvb.at[d * nz + z_])
        add_into(p, z_, b, others, cond)
        if sign >= 0:
            got(recvl.at[z_], base_l + z_, both(cond, down))
            add_into(p, z_, b, [recvl.at[z_]], both(cond, down))
        if sign <= 0:
            got(recvr.at[z_], base_r + z_, both(cond, up))
            add_into(p, z_, b, [recvr.at[z_]], both(cond, up))
        if sign > 0:
            send_sum(piece(p, z_, b), recvl.at[z_], base_l + z_, device(z + 1, b, a), cond)
        if sign < 0:
            send_sum(piece(p, z_, b), recvr.at[z_], base_r + z_, device(z - 1, b, a), cond)
    for d, a_ in enumerate(a_peers):
        send_sum(part.at[place(p, z, b, a_)], recva.at[d], base_a + d, device(z, b, a_))
    total = part[own].astype(F32)
    for d in range(na - 1):
        got(recva.at[d], base_a + d)
        total = total + recva[d].astype(F32)
    out[...] = total.astype(BF16)
    for cond, copy in sent:
        run(cond, copy.wait_send)


def per_device(lay, experts, tokens, ids, rw, wg, wu, wd, sg, su, sd):
    rows, width = tokens.shape
    nz, na, nb = lay.nz, lay.na, lay.nb
    piece = (na, rows, width)
    count = 2 * lay.n_tensor
    hidden, shared = wg.shape[2], sg.shape[1]
    per = min(lay.half, max(1, 256 // rows))
    while lay.half % per:
        per -= 1
    sends = (na - 1) + (na * (2 * nz - 1)) * (2 + nb) + (nb - 1) * na * (2 * nz - 1) + 8
    red = nz * nb + (2 * nz - 1) * nb + 2 * nz + na + 8
    vmem = pl.BlockSpec(memory_space=pltpu.VMEM)
    anyw = pl.BlockSpec(memory_space=pl.ANY)
    scratch = [
        pltpu.VMEM((lay.blocks, rows, width + lanes_for(experts)), BF16),
        pltpu.VMEM((lay.blocks, rows, width), BF16),
        pltpu.VMEM((nz * nb,) + piece, BF16),
        pltpu.VMEM((max(1, (nb - 1) * nz),) + piece, BF16),
        pltpu.VMEM((nz,) + piece, BF16),
        pltpu.VMEM((nz,) + piece, BF16),
        pltpu.VMEM((max(1, na - 1), rows, width), BF16),
        pltpu.VMEM((count, rows, width), BF16),
        pltpu.VMEM((per * rows, hidden), BF16),
        pltpu.VMEM((count * rows, shared), BF16),
        pltpu.VMEM(wg.shape[1:], BF16),
        pltpu.VMEM(wu.shape[1:], BF16),
        pltpu.VMEM(wd.shape[1:], BF16),
        pltpu.VMEM(sg.shape, BF16),
        pltpu.VMEM(su.shape, BF16),
        pltpu.VMEM(sd.shape, BF16),
        pltpu.SemaphoreType.DMA((7,)),
        pltpu.SemaphoreType.DMA((sends,)),
        pltpu.SemaphoreType.DMA((lay.blocks,)),
        pltpu.SemaphoreType.DMA((red,)),
        pltpu.SemaphoreType.DMA((nz * nb + (nb - 1) * nz + 2 * nz + na,)),
    ]
    return pl.pallas_call(
        functools.partial(kernel, lay, experts),
        out_shape=jax.ShapeDtypeStruct((rows, width), BF16),
        in_specs=[anyw, vmem, vmem] + [anyw] * 6,
        out_specs=vmem,
        scratch_shapes=scratch,
        compiler_params=pltpu.CompilerParams(
            collective_id=0, has_side_effects=True, vmem_limit_bytes=67043328
        ),
    )(tokens, ids, rw, wg, wu, wd, sg, su, sd)


def solution(mesh):
    shape = dict(mesh.shape)

    def body(tokens, ids, rw, wg, wu, wd, sg, su, sd):
        lay = Layout(shape["expert"], shape["tensor"], shape["pair"], tokens.shape[0])
        experts = shape["expert"] * shape["pair"] * wg.shape[0]
        return per_device(lay, experts, tokens, ids, rw, wg, wu, wd, sg, su, sd)

    in_specs = (
        P(("groups", "expert", "tensor", "pair"), None),
        P(("groups", "expert", "tensor", "pair"), None),
        P(("groups", "expert", "tensor", "pair"), None),
        P(("expert", "pair"), None, "tensor"),
        P(("expert", "pair"), None, "tensor"),
        P(("expert", "pair"), "tensor", None),
        P(None, ("tensor", "pair")),
        P(None, ("tensor", "pair")),
        P(("tensor", "pair"), None),
    )
    out_specs = P(("groups", "expert", "tensor", "pair"), None)
    return jax.shard_map(body, mesh=mesh, in_specs=in_specs, out_specs=out_specs, check_vma=False)
```

time: 214 us -> 76.3 us (0.36)
  blocking collectives: 119 us -> 0 us
  Pallas kernels: 0 us -> 71 us
  waiting for transfers between devices: 45.4 us -> 0 us
  matrix products: 25.7 us -> 0 us
  between operations: 13.5 us -> 0.01 us
  starting transfers between devices: 3.71 us -> 0 us
  other arithmetic: 3.18 us -> 0 us
    all_to_all x1 -> x0, blocking collectives: 90.2 us -> none  [per_device(): lax.all_to_all(copies, ('expert', 'tensor', 'pair'), split_axis=0, concat...]
    pallas_call x0 -> x1, Pallas kernels: none -> 71 us  [per_device(): pl.pallas_call(functools.partial(kernel, lay, experts), out_shape=jax.Sha...]
    all_to_all x1 -> x0, waiting for transfers between devices: 45.4 us -> none  [per_device(): lax.all_to_all(partial_value, ('expert', 'tensor', 'pair'), split_axis=0,...]
    all_gather x1 -> x0, blocking collectives: 28.8 us -> none  [per_device(): row_piece = lax.all_gather(tokens, ('tensor', 'pair'), axis=0, tiled=True)]
    dot_general x6 -> x0, matrix products: 25.7 us -> none  [the longest x1 10 us: per_device(): jnp.dot(hidden, w_down[0], preferred_element_type=jnp.float32)]
    all_to_all x1 -> x0, starting transfers between devices: 3.67 us -> none  [per_device(): lax.all_to_all(partial_value, ('expert', 'tensor', 'pair'), split_axis=0,...]
    reduce_sum x2 -> x0, other arithmetic: 3.03 us -> none  [the longest x1 2.92 us: per_device(): jnp.sum(grouped, axis=1).reshape(n_expert * n_pair, slot_count, model_width)]
  transfers between devices with their start and end apart: 2 -> 0, of which waited for: 1 -> 0; matrix products, arithmetic and copies ran while one was open for 5% -> 0% of each run, Pallas kernels for 0% -> 0%
where the time goes in v1:
time: 76.3 us; the launch traced here: 75.3 us
  Pallas kernels  71 us (93%)
  local copies, waits for them, and re-layouts  4.26 us (6%)
    pallas_call x1, Pallas kernels, per_device(): pl.pallas_call(functools.partial(kernel, lay, experts), out_shape=jax.Sha...  71 us
    unnamed x3, local copies, waits for them, and re-layouts  4.26 us

profile of v1, /device:TPU:0, one launch (start us, length us, event | category | flops | bytes accessed | tf_op | source)
XLA Modules:
  0.0 75.3 jit_solution(8104067473945413986)
XLA Ops:
  0.0 1.4 %copy.10.ids = s32[16,8]{1,0:T(8,128)} copy(s32[16,8]{0,1:T(8,128)} %param.10) | data formatting | bytes 1024 | tf_op args[1]
  1.4 1.4 %copy.11.rw = f32[16,8]{1,0:T(8,128)} copy(f32[16,8]{0,1:T(8,128)} %param.11) | data formatting | bytes 1024 | tf_op args[2]
  2.7 71.0 %shard_map.91 = bf16[16,3584]{1,0:T(8,128)(2,1)} custom-call(bf16[16,3584]{1,0:T(8,128)(2,1)} %tok_in.1, s32[16,8]{1,0:T(8,128)} %copy.10.ids, f32[16,8]{1,0:T(8,128)} %copy.11.rw, bf16[1,3584,512]{2,1,0:T(8,128)(2,1)} %wg_in.1, bf16[1,3584,512]{2,1,0:T(8,128)(2,1)} %wu_in.1, bf16[1,512,3584]{2,1,0:T(8,128)(2,1)} %wd_in.1, bf16[3584,512]{1,0:T(8,128)(2,1)} %sg_in.1, ...), custom_call_target="tpu_custom_call" | custom-call | tf_op jit(solution)/shard_map/pallas_call | solution.py:363
  73.7 1.6 %copy.13 = bf16[16,3584]{1,0:T(8,128)(2,1)} copy(bf16[16,3584]{1,0:T(8,128)(2,1)} %shard_map.91) | data formatting | bytes 229376

commit v2 on v1

v2 whole, which is shorter than its diff:
```python
import functools

import jax
import jax.numpy as jnp
from jax import lax
from jax.experimental import pallas as pl
from jax.experimental.pallas import tpu as pltpu
from jax.sharding import PartitionSpec as P

MESH = pl.DeviceIdType.MESH
F32 = jnp.float32
BF16 = jnp.bfloat16


def lanes_for(experts):
    return -(-3 * experts // 128) * 128


def tile_of(width, most):
    for tile in range(min(width, most), 0, -1):
        if width % tile == 0 and (tile % 128 == 0 or tile == width):
            return tile
    return width


class Layout:
    def __init__(self, n_expert, n_tensor, n_pair, tok_rows):
        self.n_expert, self.n_tensor, self.n_pair = n_expert, n_tensor, n_pair
        self.ny = 2 if n_expert % 2 == 0 else 1
        self.nz = n_expert // self.ny
        self.half = n_expert * n_tensor
        self.blocks = 2 * self.half
        self.rows = tok_rows
        self.first = (n_tensor, self.ny)
        self.last = (self.ny, n_tensor)

    def steps(self, z):
        out = [[(z, None)]]
        for k in range(1, self.nz):
            out.append([(z + k, z + k < self.nz), (z - k, z - k >= 0)])
        return out


def kernel(lay, experts, tok_in, ids_in, rw_in, wg_in, wu_in, wd_in, sg_in, su_in, sd_in, out,
           tok, part, ids, rw, recvp, recvb0, recvb1, recva0, recva1, recvz, xs, hid, hs,
           wg, wu, wd, sg, su, sd, load_sem, tok_send, tok_recv, red_send, red_recv):
    nz, ny, nt = lay.nz, lay.ny, lay.n_tensor
    rows, half = lay.rows, lay.half
    width = part.shape[-1]
    e_idx, t, p = lax.axis_index("expert"), lax.axis_index("tensor"), lax.axis_index("pair")
    z, y = e_idx // ny, e_idx % ny

    def device(z_, y_, t_):
        return {"expert": z_ * ny + y_, "tensor": t_, "pair": p}

    partner = {"expert": e_idx, "tensor": t, "pair": 1 - p}
    t_peers = [(t + d) % nt for d in range(1, nt)]
    y_peers = [(y + d) % ny for d in range(1, ny)]
    z_peers = [(z + d) % nz for d in range(1, nz)]

    def place(q, z_, y_, t_):
        return ((q * nz + z_) * ny + y_) * nt + t_

    cut = width // 256 * 128
    wide = (pl.ds(0, cut), pl.ds(cut, tok.shape[-1] - cut))
    cols2 = (pl.ds(0, cut), pl.ds(cut, width - cut))
    first_peers, last_peers = (t_peers, y_peers), (y_peers, t_peers)
    first_at, last_at = (t, y), (y, t)

    def yt(h, first_, last_):
        return (last_, first_) if h == 0 else (first_, last_)

    own = place(p, z, y, t)
    first = pltpu.make_async_copy(tok_in, tok.at[own, :, pl.ds(0, width)], load_sem.at[6])
    first.start()
    small = [pltpu.make_async_copy(ids_in, ids, load_sem.at[7]), pltpu.make_async_copy(rw_in, rw, load_sem.at[8])]
    for load in small:
        load.start()
    loads = [
        pltpu.make_async_copy(src, dst, load_sem.at[i])
        for i, (src, dst) in enumerate(
            ((sg_in, sg), (su_in, su), (sd_in, sd), (wg_in.at[0], wg), (wu_in.at[0], wu), (wd_in.at[0], wd))
        )
    ]
    for load in loads:
        load.start()

    barrier = pltpu.get_barrier_semaphore()

    def greet(dev):
        pl.semaphore_signal(barrier, inc=1, device_id=dev, device_id_type=MESH)

    greet(partner)
    for t_ in t_peers:
        greet(device(z, y, t_))
    for y_ in y_peers:
        greet(device(z, y_, t))
    for z_ in z_peers:
        greet(device(z_, y, t))

    for load in small:
        load.wait()
    lane = lax.broadcasted_iota(jnp.int32, (rows, tok.shape[-1] - width), 1)
    top = ids.shape[1]
    pieces = [jnp.zeros(lane.shape, F32) for _ in range(3)]
    for k in range(top):
        for m in range(3):
            pieces[m] = pieces[m] + jnp.where(lane == ids[:, k : k + 1] + m * experts, rw[:, k : k + 1], 0.0)
    hi = [v.astype(BF16).astype(F32) for v in pieces]
    rest = [v - h for v, h in zip(pieces, hi)]
    mid = [v.astype(BF16).astype(F32) for v in rest]
    low = [v - h for v, h in zip(rest, mid)]
    tok[own, :, pl.ds(width, lane.shape[1])] = (hi[0] + mid[1] + low[2]).astype(BF16)

    pl.semaphore_wait(barrier, nt + ny + nz - 2)

    first.wait()

    sent = []

    def both(c1, c2):
        return c2 if c1 is None else (c1 if c2 is None else jnp.logical_and(c1, c2))

    def run(cond, fn):
        if cond is None:
            fn()
        else:
            pl.when(cond)(fn)

    def send(src, dst, sem_send, sem_recv, dev, cond=None):
        copy = pltpu.make_async_remote_copy(
            src_ref=src, dst_ref=dst, send_sem=sem_send, recv_sem=sem_recv,
            device_id=dev, device_id_type=MESH)
        run(cond, copy.start)
        sent.append((cond, copy))

    counter = [0]

    def send_block(h, idx, dev, cond=None):
        view = tok.at[idx, :, wide[h]]
        send(view, view, tok_send.at[counter[0]], tok_recv.at[h, idx], dev, cond)
        counter[0] += 1

    def arrive(h, idx, cond=None):
        view = tok.at[idx, :, wide[h]]
        copy = pltpu.make_async_remote_copy(
            src_ref=view, dst_ref=view, send_sem=tok_send.at[0],
            recv_sem=tok_recv.at[h, idx], device_id=partner, device_id_type=MESH)
        run(cond, copy.wait_recv)

    def last_sends(h, idx, cond):
        for v in last_peers[h]:
            send_block(h, idx, device(z, *yt(h, first_at[h], v)), cond)

    def stage_line(k):
        for z_, cond in line[k]:
            blk = place(p, z_, y, t)
            for h in range(2):
                if k:
                    arrive(h, blk, cond)
                for v in first_peers[h]:
                    send_block(h, blk, device(z, *yt(h, v, last_at[h])), cond)
            for h in range(2):
                last_sends(h, blk, cond)
                send_block(h, blk, partner, cond)

    def stage_first(k):
        for z_, cond in line[k]:
            for d in range(max(ny, nt) - 1):
                for h in range(2):
                    if d < len(first_peers[h]):
                        blk = place(p, z_, *yt(h, first_peers[h][d], last_at[h]))
                        arrive(h, blk, cond)
                        last_sends(h, blk, cond)
                        send_block(h, blk, partner, cond)

    def stage_last(k):
        for z_, cond in line[k]:
            for h in range(2):
                for f in [first_at[h]] + first_peers[h]:
                    for v in last_peers[h]:
                        blk = place(p, z_, *yt(h, f, v))
                        arrive(h, blk, cond)
                        send_block(h, blk, partner, cond)

    line = lay.steps(z)
    for k in range(1, nz):
        for z_, cond in line[k]:
            for h in range(2):
                send_block(h, own, device(z_, y, t), cond)
    for k in range(nz + 2):
        if k < nz:
            stage_line(k)
        if 0 <= k - 1 < nz:
            stage_first(k - 1)
        if 0 <= k - 2 < nz:
            stage_last(k - 2)
    for k in range(nz):
        for z_, cond in line[k]:
            for y_ in range(ny):
                for t_ in range(nt):
                    for h in range(2):
                        arrive(h, place(1 - p, z_, y_, t_), cond)

    group = []
    for q in range(2):
        for t_ in range(lay.n_tensor):
            group.append(place(q, z, y, t_))
    for i, idx in enumerate(group):
        xs[i] = tok[idx, :, pl.ds(0, width)]
    count = len(group)

    def hidden_tiles(x, w1, w2, scale, store):
        tile = tile_of(w1.shape[1], 256)

        def body(n, _):
            cols = pl.ds(pl.multiple_of(n * tile, tile), tile)
            g = jnp.dot(x(), w1[:, cols], preferred_element_type=F32)
            u = jnp.dot(x(), w2[:, cols], preferred_element_type=F32)
            h = g / (1.0 + jnp.exp(-g)) * u
            if scale is not None:
                h = h * scale
            store[:, cols] = h.astype(BF16)
            return 0

        lax.fori_loop(0, w1.shape[1] // tile, body, 0)

    loads[0].wait()
    loads[1].wait()
    hidden_tiles(lambda: xs[...].reshape(count * rows, width), sg, su, None, hs)
    loads[2].wait()
    for i in range(3, 6):
        loads[i].wait()

    out_tile = tile_of(width, 512)
    per = min(half, max(1, 256 // rows))
    while half % per:
        per -= 1
    mine = e_idx * lay.n_pair + p

    def chunk(c, _):
        at = c * per
        extra = tok[pl.ds(at, per), :, pl.ds(width, lane.shape[1])].reshape(per * rows, lane.shape[1])
        l2 = lax.broadcasted_iota(jnp.int32, extra.shape, 1)
        pick = (l2 == mine) | (l2 == mine + experts) | (l2 == mine + 2 * experts)
        scale = jnp.sum(jnp.where(pick, extra.astype(F32), 0.0), axis=1, keepdims=True)
        hidden_tiles(lambda: tok[pl.ds(at, per), :, pl.ds(0, width)].reshape(per * rows, width), wg, wu, scale, hid)

        def body(n, _):
            cols = pl.ds(pl.multiple_of(n * out_tile, out_tile), out_tile)
            v = jnp.dot(hid[...], wd[:, cols], preferred_element_type=F32)
            part[pl.ds(at, per), :, cols] = v.astype(BF16).reshape(per, rows, out_tile)
            return 0

        lax.fori_loop(0, width // out_tile, body, 0)
        return 0

    def shared_into(q):
        lo = q * (count // 2)

        def body(n, _):
            cols = pl.ds(pl.multiple_of(n * out_tile, out_tile), out_tile)
            r0 = pl.multiple_of(lo * rows, rows)
            v = jnp.dot(hs[pl.ds(r0, count // 2 * rows), :], sd[:, cols], preferred_element_type=F32)
            for j in range(count // 2):
                idx = place(q, z, y, j)
                part[idx, :, cols] = (part[idx, :, cols].astype(F32) + v[j * rows : (j + 1) * rows]).astype(BF16)
            return 0

        lax.fori_loop(0, width // out_tile, body, 0)

    rcount = [0]

    def send_sum(src, dst, recv_at, dev, cond=None):
        send(src, dst, red_send.at[rcount[0]], red_recv.at[recv_at], dev, cond)
        rcount[0] += 1

    def got(dst, recv_at, cond=None):
        copy = pltpu.make_async_remote_copy(
            src_ref=dst, dst_ref=dst, send_sem=red_send.at[0], recv_sem=red_recv.at[recv_at],
            device_id=partner, device_id_type=MESH)
        run(cond, copy.wait_recv)

    steps = half // per
    other = 1 - p
    lax.fori_loop(0, steps, lambda c, v: chunk(other * steps + c, v), 0)
    shared_into(other)

    recvb, recva = (recvb0, recvb1), (recva0, recva1)
    base = [half]
    bases = {}

    def at(kind, h, n):
        if (kind, h) not in bases:
            bases[kind, h] = base[0]
            base[0] += n
        return bases[kind, h]

    far = [pair for k in range(nz - 1, -1, -1) for pair in line[k]]

    for y_ in range(ny):
        for z_ in range(nz):
            at_ = z_ * ny + y_
            send_sum(part.at[pl.ds(place(other, z_, y_, 0), nt)], recvp.at[pl.ds(at_ * nt, nt)], at_, partner)
    lax.fori_loop(0, steps, lambda c, v: chunk(p * steps + c, v), 0)
    shared_into(p)

    def buf_b(h, d, z_, f):
        n = lay.first[h]
        at_ = (d * nz + z_) * n + f
        return recvb[h].at[at_], at("b", h, (lay.last[h] - 1) * nz * n) + at_

    def buf_a(h, d, z_):
        return recva[h].at[d * nz + z_], at("a", h, (lay.first[h] - 1) * nz) + d * nz + z_

    def buf_z(h, d):
        return recvz.at[d, :, cols2[h]], at("z", h, nz - 1) + d

    def add_into(h, idx, others, cond):
        def fn():
            v = part[idx, :, cols2[h]].astype(F32)
            for ref in others:
                v = v + ref[...].astype(F32)
            part[idx, :, cols2[h]] = v.astype(BF16)
        run(cond, fn)

    def mine_of(z_, y_, t_, h):
        return recvp.at[(z_ * ny + y_) * nt + t_, :, cols2[h]]

    def sums_last(z_, cond):
        for y_ in [(y + 1 + d) % ny for d in range(ny)]:
            got(recvp.at[pl.ds((z_ * ny + y_) * nt, nt)], z_ * ny + y_, cond)
        for f in range(max(ny, nt) - 1, -1, -1):
            for h in range(2):
                firsts = [first_at[h]] + first_peers[h]
                if f >= len(firsts):
                    continue
                for d, v in enumerate(last_peers[h]):
                    y_, t_ = yt(h, firsts[f], v)
                    idx = place(p, z_, y_, t_)
                    add_into(h, idx, [mine_of(z_, y_, t_, h)], cond)
                    ref, sem = buf_b(h, d, z_, firsts[f])
                    y2, t2 = yt(h, first_at[h], v)
                    send_sum(part.at[idx, :, cols2[h]], ref, sem, device(z, y2, t2), cond)

    def collect_last(h, z_, f, cond):
        y_, t_ = yt(h, f, last_at[h])
        refs = [mine_of(z_, y_, t_, h)]
        for d in range(lay.last[h] - 1):
            ref, sem = buf_b(h, d, z_, f)
            got(ref, sem, cond)
            refs.append(ref)
        return place(p, z_, y_, t_), refs

    def sums_first(z_, cond):
        for h in range(2):
            for d, f in enumerate(first_peers[h]):
                idx, refs = collect_last(h, z_, f, cond)
                add_into(h, idx, refs, cond)
                ref, sem = buf_a(h, d, z_)
                send_sum(part.at[idx, :, cols2[h]], ref, sem, device(z, *yt(h, f, last_at[h])), cond)

    def sums_line(z_, cond):
        for h in range(2):
            idx, refs = collect_last(h, z_, first_at[h], cond)
            for d in range(lay.first[h] - 1):
                ref, sem = buf_a(h, d, z_)
                got(ref, sem, cond)
                refs.append(ref)
            if cond is None:
                for d in range(nz - 1):
                    ref, sem = buf_z(h, d)
                    got(ref, sem)
                    refs.append(ref)
            add_into(h, idx, refs, cond)
            if cond is not None:
                d = (z_ - z + nz) % nz - 1
                ref, sem = buf_z(h, d)
                send_sum(part.at[idx, :, cols2[h]], ref, sem, device(z_, y, t), cond)

    for i in range(len(far) + 4):
        if i < len(far):
            sums_last(*far[i])
        if 0 <= i - 2 < len(far):
            sums_first(*far[i - 2])
        if 0 <= i - 4 < len(far):
            sums_line(*far[i - 4])
    total = part[own]
    out[...] = total
    for cond, copy in sent:
        run(cond, copy.wait_send)


def per_device(lay, experts, tokens, ids, rw, wg, wu, wd, sg, su, sd):
    rows, width = tokens.shape
    nz, ny, nt = lay.nz, lay.ny, lay.n_tensor
    cut = width // 256 * 128
    count = 2 * lay.n_tensor
    hidden, shared = wg.shape[2], sg.shape[1]
    per = min(lay.half, max(1, 256 // rows))
    while lay.half % per:
        per -= 1
    span = 2 * nz - 1
    sends = 4 * (nz - 1) + span * (nt - 1 + ny - 1) + 2 * span * (nt * ny) + span * 2 * nt * ny
    red = nz * ny + 2 * span * nt * ny + 4 * nz + 2 * span * (nt + ny)
    halves = (cut, width - cut)
    many_b = [max(1, (lay.last[h] - 1) * nz * lay.first[h]) for h in range(2)]
    many_a = [max(1, (lay.first[h] - 1) * nz) for h in range(2)]
    vmem = pl.BlockSpec(memory_space=pltpu.VMEM)
    anyw = pl.BlockSpec(memory_space=pl.ANY)
    scratch = [
        pltpu.VMEM((lay.blocks, rows, width + lanes_for(experts)), BF16),
        pltpu.VMEM((lay.blocks, rows, width), BF16),
        pltpu.VMEM(ids.shape, jnp.int32),
        pltpu.VMEM(rw.shape, F32),
        pltpu.VMEM((lay.half, rows, width), BF16),
        pltpu.VMEM((many_b[0], rows, halves[0]), BF16),
        pltpu.VMEM((many_b[1], rows, halves[1]), BF16),
        pltpu.VMEM((many_a[0], rows, halves[0]), BF16),
        pltpu.VMEM((many_a[1], rows, halves[1]), BF16),
        pltpu.VMEM((max(1, nz - 1), rows, width), BF16),
        pltpu.VMEM((count, rows, width), BF16),
        pltpu.VMEM((per * rows, hidden), BF16),
        pltpu.VMEM((count * rows, shared), BF16),
        pltpu.VMEM(wg.shape[1:], BF16),
        pltpu.VMEM(wu.shape[1:], BF16),
        pltpu.VMEM(wd.shape[1:], BF16),
        pltpu.VMEM(sg.shape, BF16),
        pltpu.VMEM(su.shape, BF16),
        pltpu.VMEM(sd.shape, BF16),
        pltpu.SemaphoreType.DMA((9,)),
        pltpu.SemaphoreType.DMA((sends,)),
        pltpu.SemaphoreType.DMA((2, lay.blocks)),
        pltpu.SemaphoreType.DMA((red,)),
        pltpu.SemaphoreType.DMA((lay.half + sum(many_b) + sum(many_a) + 2 * nz,)),
    ]
    return pl.pallas_call(
        functools.partial(kernel, lay, experts),
        out_shape=jax.ShapeDtypeStruct((rows, width), BF16),
        in_specs=[anyw] * 9,
        out_specs=vmem,
        scratch_shapes=scratch,
        compiler_params=pltpu.CompilerParams(
            collective_id=0, has_side_effects=True, vmem_limit_bytes=67043328
        ),
    )(tokens, ids, rw, wg, wu, wd, sg, su, sd)


def solution(mesh):
    shape = dict(mesh.shape)

    def body(tokens, ids, rw, wg, wu, wd, sg, su, sd):
        lay = Layout(shape["expert"], shape["tensor"], shape["pair"], tokens.shape[0])
        experts = shape["expert"] * shape["pair"] * wg.shape[0]
        return per_device(lay, experts, tokens, ids, rw, wg, wu, wd, sg, su, sd)

    in_specs = (
        P(("groups", "expert", "tensor", "pair"), None),
        P(("groups", "expert", "tensor", "pair"), None),
        P(("groups", "expert", "tensor", "pair"), None),
        P(("expert", "pair"), None, "tensor"),
        P(("expert", "pair"), None, "tensor"),
        P(("expert", "pair"), "tensor", None),
        P(None, ("tensor", "pair")),
        P(None, ("tensor", "pair")),
        P(("tensor", "pair"), None),
    )
    out_specs = P(("groups", "expert", "tensor", "pair"), None)
    return jax.shard_map(body, mesh=mesh, in_specs=in_specs, out_specs=out_specs, check_vma=False)
```

time: 76.3 us -> 68.6 us (0.90); the launches traced: 75.3 us -> 68.3 us
  Pallas kernels: 71 us -> 64.1 us
    pallas_call x1, Pallas kernels: 71 us -> 64.1 us  [per_device(): pl.pallas_call(functools.partial(kernel, lay, experts), out_shape=jax.Sha...]
where the time goes in v2:
time: 68.6 us; the launch traced here: 68.3 us
  Pallas kernels  64.1 us (93%)
  local copies, waits for them, and re-layouts  4.26 us (6%)
    pallas_call x1, Pallas kernels, per_device(): pl.pallas_call(functools.partial(kernel, lay, experts), out_shape=jax.Sha...  64.1 us
    unnamed x3, local copies, waits for them, and re-layouts  4.26 us

profile of v2, /device:TPU:0, one launch (start us, length us, event | category | flops | bytes accessed | tf_op | source)
XLA Modules:
  0.0 68.3 jit_solution(8721064974502658171)
XLA Ops:
  0.0 1.4 %copy.10.ids_in = s32[16,8]{1,0:T(8,128)} copy(s32[16,8]{0,1:T(8,128)} %param.10) | data formatting | bytes 1024 | tf_op args[1]
  1.4 1.4 %copy.11.rw_in = f32[16,8]{1,0:T(8,128)} copy(f32[16,8]{0,1:T(8,128)} %param.11) | data formatting | bytes 1024 | tf_op args[2]
  2.7 64.1 %shard_map.91 = bf16[16,3584]{1,0:T(8,128)(2,1)} custom-call(bf16[16,3584]{1,0:T(8,128)(2,1)} %tok_in.1, s32[16,8]{1,0:T(8,128)} %copy.10.ids_in, f32[16,8]{1,0:T(8,128)} %copy.11.rw_in, bf16[1,3584,512]{2,1,0:T(8,128)(2,1)} %wg_in.1, bf16[1,3584,512]{2,1,0:T(8,128)(2,1)} %wu_in.1, bf16[1,512,3584]{2,1,0:T(8,128)(2,1)} %wd_in.1, bf16[3584,512]{1,0:T(8,128)(2,1)} %sg_in.1, ...), custom_call_target="tpu_custom_call" | custom-call | tf_op jit(solution)/shard_map/pallas_call | solution.py:437
  66.8 1.6 %copy.13 = bf16[16,3584]{1,0:T(8,128)(2,1)} copy(bf16[16,3584]{1,0:T(8,128)(2,1)} %shard_map.91) | data formatting | bytes 229376

commit v3 on v2

--- a/solution.py
+++ b/solution.py
@@ -21,6 +21,13 @@
         if width % tile == 0 and (tile % 128 == 0 or tile == width):
             return tile
     return width
+
+
+def part_rows(span, rows):
+    per = min(span, max(1, 256 // rows))
+    while span % per:
+        per -= 1
+    return per
 
 
 class Layout:
@@ -34,15 +41,18 @@
         self.first = (n_tensor, self.ny)
         self.last = (self.ny, n_tensor)
 
-    def steps(self, z):
-        out = [[(z, None)]]
-        for k in range(1, self.nz):
-            out.append([(z + k, z + k < self.nz), (z - k, z - k >= 0)])
-        return out
+    def near_far(self, z):
+        if self.nz % 2:
+            return [z] + [(z + d) % self.nz for d in range(1, self.nz)], []
+        hz = self.nz // 2
+        zh = z // hz
+        near = [z] + [zh * hz + (z + d) % hz for d in range(1, hz)]
+        far = [(hz + d) * (1 - zh) + (hz - 1 - d) * zh for d in range(hz)]
+        return near, far
 
 
 def kernel(lay, experts, tok_in, ids_in, rw_in, wg_in, wu_in, wd_in, sg_in, su_in, sd_in, out,
-           tok, part, ids, rw, recvp, recvb0, recvb1, recva0, recva1, recvz, xs, hid, hs,
+           tok, part, ids, rw, recvp, recvb0, recvb1, recva0, recva1, recvz0, recvz1, xs, hid, hs,
            wg, wu, wd, sg, su, sd, load_sem, tok_send, tok_recv, red_send, red_recv):
     nz, ny, nt = lay.nz, lay.ny, lay.n_tensor
     rows, half = lay.rows, lay.half
@@ -136,71 +146,74 @@
 
     counter = [0]
 
-    def send_block(h, idx, dev, cond=None):
+    def send_block(h, idx, dev):
         view = tok.at[idx, :, wide[h]]
-        send(view, view, tok_send.at[counter[0]], tok_recv.at[h, idx], dev, cond)
+        send(view, view, tok_send.at[counter[0]], tok_recv.at[h, idx], dev)
         counter[0] += 1
 
-    def arrive(h, idx, cond=None):
+    def arrive(h, idx):
         view = tok.at[idx, :, wide[h]]
-        copy = pltpu.make_async_remote_copy(
+        pltpu.make_async_remote_copy(
             src_ref=view, dst_ref=view, send_sem=tok_send.at[0],
-            recv_sem=tok_recv.at[h, idx], device_id=partner, device_id_type=MESH)
-        run(cond, copy.wait_recv)
-
-    def last_sends(h, idx, cond):
+            recv_sem=tok_recv.at[h, idx], device_id=partner, device_id_type=MESH).wait_recv()
+
+    near, far = lay.near_far(z)
+
+    def last_sends(h, idx, f):
         for v in last_peers[h]:
-            send_block(h, idx, device(z, *yt(h, first_at[h], v)), cond)
-
-    def stage_line(k):
-        for z_, cond in line[k]:
-            blk = place(p, z_, y, t)
+            send_block(h, idx, device(z, *yt(h, f, v)))
+        send_block(h, idx, partner)
+
+    def line_sends(h, idx):
+        for z_ in near[1:] + far:
+            send_block(h, idx, device(z_, y, t))
+
+    for h in range(2):
+        for f in first_peers[h]:
+            send_block(h, own, device(z, *yt(h, f, last_at[h])))
+    for h in range(2):
+        line_sends(h, own)
+    for h in range(2):
+        last_sends(h, own, first_at[h])
+    for d in range(max(ny, nt) - 1):
+        for h in range(2):
+            if d < len(first_peers[h]):
+                blk = place(p, z, *yt(h, first_peers[h][d], last_at[h]))
+                arrive(h, blk)
+                line_sends(h, blk)
+                last_sends(h, blk, first_at[h])
+
+    def stage_line(z_):
+        for d in range(max(ny, nt)):
             for h in range(2):
-                if k:
-                    arrive(h, blk, cond)
-                for v in first_peers[h]:
-                    send_block(h, blk, device(z, *yt(h, v, last_at[h])), cond)
-            for h in range(2):
-                last_sends(h, blk, cond)
-                send_block(h, blk, partner, cond)
-
-    def stage_first(k):
-        for z_, cond in line[k]:
-            for d in range(max(ny, nt) - 1):
+                firsts = [first_at[h]] + first_peers[h]
+                if d < len(firsts):
+                    blk = place(p, z_, *yt(h, firsts[d], last_at[h]))
+                    arrive(h, blk)
+                    last_sends(h, blk, first_at[h])
+
+    def stage_last(z_):
+        for h in range(2):
+            for f in [first_at[h]] + first_peers[h]:
+                for v in last_peers[h]:
+                    blk = place(p, z_, *yt(h, f, v))
+                    arrive(h, blk)
+                    send_block(h, blk, partner)
+
+    def stage_partner(z_):
+        for y_ in range(ny):
+            for t_ in range(nt):
                 for h in range(2):
-                    if d < len(first_peers[h]):
-                        blk = place(p, z_, *yt(h, first_peers[h][d], last_at[h]))
-                        arrive(h, blk, cond)
-                        last_sends(h, blk, cond)
-                        send_block(h, blk, partner, cond)
-
-    def stage_last(k):
-        for z_, cond in line[k]:
-            for h in range(2):
-                for f in [first_at[h]] + first_peers[h]:
-                    for v in last_peers[h]:
-                        blk = place(p, z_, *yt(h, f, v))
-                        arrive(h, blk, cond)
-                        send_block(h, blk, partner, cond)
-
-    line = lay.steps(z)
-    for k in range(1, nz):
-        for z_, cond in line[k]:
-            for h in range(2):
-                send_block(h, own, device(z_, y, t), cond)
-    for k in range(nz + 2):
-        if k < nz:
-            stage_line(k)
-        if 0 <= k - 1 < nz:
-            stage_first(k - 1)
-        if 0 <= k - 2 < nz:
-            stage_last(k - 2)
-    for k in range(nz):
-        for z_, cond in line[k]:
-            for y_ in range(ny):
-                for t_ in range(nt):
-                    for h in range(2):
-                        arrive(h, place(1 - p, z_, y_, t_), cond)
+                    arrive(h, place(1 - p, z_, y_, t_))
+
+    for z_ in near[1:]:
+        stage_line(z_)
+    for z_ in near:
+        stage_last(z_)
+    for z_ in far:
+        stage_line(z_)
+    for z_ in near:
+        stage_partner(z_)
 
     group = []
     for q in range(2):
@@ -225,21 +238,12 @@
 
         lax.fori_loop(0, w1.shape[1] // tile, body, 0)
 
-    loads[0].wait()
-    loads[1].wait()
-    hidden_tiles(lambda: xs[...].reshape(count * rows, width), sg, su, None, hs)
-    loads[2].wait()
-    for i in range(3, 6):
-        loads[i].wait()
-
     out_tile = tile_of(width, 512)
-    per = min(half, max(1, 256 // rows))
-    while half % per:
-        per -= 1
+    span = half * len(near) // nz
+    per = part_rows(span, rows)
     mine = e_idx * lay.n_pair + p
 
-    def chunk(c, _):
-        at = c * per
+    def rows_of(at):
         extra = tok[pl.ds(at, per), :, pl.ds(width, lane.shape[1])].reshape(per * rows, lane.shape[1])
         l2 = lax.broadcasted_iota(jnp.int32, extra.shape, 1)
         pick = (l2 == mine) | (l2 == mine + experts) | (l2 == mine + 2 * experts)
@@ -253,7 +257,6 @@
             return 0
 
         lax.fori_loop(0, width // out_tile, body, 0)
-        return 0
 
     def shared_into(q):
         lo = q * (count // 2)
@@ -281,12 +284,25 @@
             device_id=partner, device_id_type=MESH)
         run(cond, copy.wait_recv)
 
-    steps = half // per
+    steps = span // per
     other = 1 - p
-    lax.fori_loop(0, steps, lambda c, v: chunk(other * steps + c, v), 0)
-    shared_into(other)
-
-    recvb, recva = (recvb0, recvb1), (recva0, recva1)
+
+    def compute(q, z_first):
+        at0 = place(q, z_first, 0, 0)
+
+        def go(c, _):
+            rows_of(at0 + c * per)
+            return 0
+
+        lax.fori_loop(0, steps, go, 0)
+
+    def partner_sums(zs):
+        for z_ in zs:
+            for y_ in range(ny):
+                at_ = z_ * ny + y_
+                send_sum(part.at[pl.ds(place(other, z_, y_, 0), nt)], recvp.at[pl.ds(at_ * nt, nt)], at_, partner)
+
+    recvb, recva, recvz = (recvb0, recvb1), (recva0, recva1), (recvz0, recvz1)
     base = [half]
     bases = {}
 
@@ -296,95 +312,113 @@
             base[0] += n
         return bases[kind, h]
 
-    far = [pair for k in range(nz - 1, -1, -1) for pair in line[k]]
-
-    for y_ in range(ny):
-        for z_ in range(nz):
-            at_ = z_ * ny + y_
-            send_sum(part.at[pl.ds(place(other, z_, y_, 0), nt)], recvp.at[pl.ds(at_ * nt, nt)], at_, partner)
-    lax.fori_loop(0, steps, lambda c, v: chunk(p * steps + c, v), 0)
-    shared_into(p)
-
     def buf_b(h, d, z_, f):
         n = lay.first[h]
         at_ = (d * nz + z_) * n + f
         return recvb[h].at[at_], at("b", h, (lay.last[h] - 1) * nz * n) + at_
 
-    def buf_a(h, d, z_):
-        return recva[h].at[d * nz + z_], at("a", h, (lay.first[h] - 1) * nz) + d * nz + z_
-
-    def buf_z(h, d):
-        return recvz.at[d, :, cols2[h]], at("z", h, nz - 1) + d
-
-    def add_into(h, idx, others, cond):
-        def fn():
-            v = part[idx, :, cols2[h]].astype(F32)
-            for ref in others:
-                v = v + ref[...].astype(F32)
-            part[idx, :, cols2[h]] = v.astype(BF16)
-        run(cond, fn)
+    def buf_a(h, d):
+        return recva[h].at[d], at("a", h, lay.first[h] - 1) + d
+
+    def buf_z(h, d, f):
+        n = lay.first[h]
+        return recvz[h].at[d * n + f], at("z", h, (nz - 1) * n) + d * n + f
+
+    def add_into(h, idx, others):
+        v = part[idx, :, cols2[h]].astype(F32)
+        for ref in others:
+            v = v + ref[...].astype(F32)
+        part[idx, :, cols2[h]] = v.astype(BF16)
 
     def mine_of(z_, y_, t_, h):
         return recvp.at[(z_ * ny + y_) * nt + t_, :, cols2[h]]
 
-    def sums_last(z_, cond):
-        for y_ in [(y + 1 + d) % ny for d in range(ny)]:
-            got(recvp.at[pl.ds((z_ * ny + y_) * nt, nt)], z_ * ny + y_, cond)
+    def sums_last(z_):
+        for y_ in range(ny):
+            got(recvp.at[pl.ds((z_ * ny + y_) * nt, nt)], z_ * ny + y_)
         for f in range(max(ny, nt) - 1, -1, -1):
             for h in range(2):
-                firsts = [first_at[h]] + first_peers[h]
+                firsts = first_peers[h] + [first_at[h]]
                 if f >= len(firsts):
                     continue
                 for d, v in enumerate(last_peers[h]):
                     y_, t_ = yt(h, firsts[f], v)
                     idx = place(p, z_, y_, t_)
-                    add_into(h, idx, [mine_of(z_, y_, t_, h)], cond)
+                    add_into(h, idx, [mine_of(z_, y_, t_, h)])
                     ref, sem = buf_b(h, d, z_, firsts[f])
                     y2, t2 = yt(h, first_at[h], v)
-                    send_sum(part.at[idx, :, cols2[h]], ref, sem, device(z, y2, t2), cond)
-
-    def collect_last(h, z_, f, cond):
+                    send_sum(part.at[idx, :, cols2[h]], ref, sem, device(z, y2, t2))
+
+    def collect_last(h, z_, f):
         y_, t_ = yt(h, f, last_at[h])
         refs = [mine_of(z_, y_, t_, h)]
         for d in range(lay.last[h] - 1):
             ref, sem = buf_b(h, d, z_, f)
-            got(ref, sem, cond)
+            got(ref, sem)
             refs.append(ref)
         return place(p, z_, y_, t_), refs
 
-    def sums_first(z_, cond):
-        for h in range(2):
-            for d, f in enumerate(first_peers[h]):
-                idx, refs = collect_last(h, z_, f, cond)
-                add_into(h, idx, refs, cond)
-                ref, sem = buf_a(h, d, z_)
-                send_sum(part.at[idx, :, cols2[h]], ref, sem, device(z, *yt(h, f, last_at[h])), cond)
-
-    def sums_line(z_, cond):
-        for h in range(2):
-            idx, refs = collect_last(h, z_, first_at[h], cond)
-            for d in range(lay.first[h] - 1):
-                ref, sem = buf_a(h, d, z_)
-                got(ref, sem, cond)
-                refs.append(ref)
-            if cond is None:
-                for d in range(nz - 1):
-                    ref, sem = buf_z(h, d)
-                    got(ref, sem)
-                    refs.append(ref)
-            add_into(h, idx, refs, cond)
-            if cond is not None:
-                d = (z_ - z + nz) % nz - 1
-                ref, sem = buf_z(h, d)
-                send_sum(part.at[idx, :, cols2[h]], ref, sem, device(z_, y, t), cond)
-
-    for i in range(len(far) + 4):
-        if i < len(far):
-            sums_last(*far[i])
-        if 0 <= i - 2 < len(far):
-            sums_first(*far[i - 2])
-        if 0 <= i - 4 < len(far):
-            sums_line(*far[i - 4])
+    def sums_line(z_):
+        for f in range(max(ny, nt) - 1, -1, -1):
+            for h in range(2):
+                firsts = first_peers[h] + [first_at[h]]
+                if f >= len(firsts):
+                    continue
+                idx, refs = collect_last(h, z_, firsts[f])
+                add_into(h, idx, refs)
+                ref, sem = buf_z(h, (z_ - z + nz) % nz - 1, firsts[f])
+                send_sum(part.at[idx, :, cols2[h]], ref, sem, device(z_, y, t))
+
+    def collect_line(h, f):
+        idx, refs = collect_last(h, z, f)
+        for d in range(nz - 1):
+            ref, sem = buf_z(h, d, f)
+            got(ref, sem)
+            refs.append(ref)
+        return idx, refs
+
+    for i in range(3, 6):
+        loads[i].wait()
+    compute(0, near[0] // len(near) * len(near))
+    compute(1, near[0] // len(near) * len(near))
+    loads[0].wait()
+    loads[1].wait()
+    hidden_tiles(lambda: xs[...].reshape(count * rows, width), sg, su, None, hs)
+    loads[2].wait()
+    shared_into(0)
+    shared_into(1)
+    partner_sums(near[::-1])
+    if far:
+        for z_ in far:
+            stage_last(z_)
+        for z_ in far:
+            stage_partner(z_)
+        far_first = (1 - near[0] // len(near)) * len(near)
+        compute(other, far_first)
+        partner_sums(far[::-1])
+        for z_ in near[::-1]:
+            sums_last(z_)
+        compute(p, far_first)
+        for z_ in far[::-1]:
+            sums_last(z_)
+    else:
+        for z_ in near[::-1]:
+            sums_last(z_)
+    for z_ in near[:0:-1] + far[::-1]:
+        sums_line(z_)
+    for h in range(2):
+        for d, f in enumerate(first_peers[h]):
+            idx, refs = collect_line(h, f)
+            add_into(h, idx, refs)
+            ref, sem = buf_a(h, d)
+            send_sum(part.at[idx, :, cols2[h]], ref, sem, device(z, *yt(h, f, last_at[h])))
+    for h in range(2):
+        idx, refs = collect_line(h, first_at[h])
+        for d in range(lay.first[h] - 1):
+            ref, sem = buf_a(h, d)
+            got(ref, sem)
+            refs.append(ref)
+        add_into(h, idx, refs)
     total = part[own]
     out[...] = total
     for cond, copy in sent:
@@ -397,15 +431,13 @@
     cut = width // 256 * 128
     count = 2 * lay.n_tensor
     hidden, shared = wg.shape[2], sg.shape[1]
-    per = min(lay.half, max(1, 256 // rows))
-    while lay.half % per:
-        per -= 1
-    span = 2 * nz - 1
-    sends = 4 * (nz - 1) + span * (nt - 1 + ny - 1) + 2 * span * (nt * ny) + span * 2 * nt * ny
-    red = nz * ny + 2 * span * nt * ny + 4 * nz + 2 * span * (nt + ny)
+    per = part_rows(lay.half // (1 if nz % 2 else 2), rows)
+    sends = 2 * (nt + ny) * nz + 4 * nz * nt * ny
+    red = nz * ny + 2 * nz * nt * ny + (nz + 1) * (nt + ny)
     halves = (cut, width - cut)
     many_b = [max(1, (lay.last[h] - 1) * nz * lay.first[h]) for h in range(2)]
-    many_a = [max(1, (lay.first[h] - 1) * nz) for h in range(2)]
+    many_a = [max(1, lay.first[h] - 1) for h in range(2)]
+    many_z = [max(1, (nz - 1) * lay.first[h]) for h in range(2)]
     vmem = pl.BlockSpec(memory_space=pltpu.VMEM)
     anyw = pl.BlockSpec(memory_space=pl.ANY)
     scratch = [
@@ -418,7 +450,8 @@
         pltpu.VMEM((many_b[1], rows, halves[1]), BF16),
         pltpu.VMEM((many_a[0], rows, halves[0]), BF16),
         pltpu.VMEM((many_a[1], rows, halves[1]), BF16),
-        pltpu.VMEM((max(1, nz - 1), rows, width), BF16),
+        pltpu.VMEM((many_z[0], rows, halves[0]), BF16),
+        pltpu.VMEM((many_z[1], rows, halves[1]), BF16),
         pltpu.VMEM((count, rows, width), BF16),
         pltpu.VMEM((per * rows, hidden), BF16),
         pltpu.VMEM((count * rows, shared), BF16),
@@ -432,7 +465,7 @@
         pltpu.SemaphoreType.DMA((sends,)),
         pltpu.SemaphoreType.DMA((2, lay.blocks)),
         pltpu.SemaphoreType.DMA((red,)),
-        pltpu.SemaphoreType.DMA((lay.half + sum(many_b) + sum(many_a) + 2 * nz,)),
+        pltpu.SemaphoreType.DMA((lay.half + sum(many_b) + sum(many_a) + sum(many_z),)),
     ]
     return pl.pallas_call(
         functools.partial(kernel, lay, experts),

time: 68.6 us -> 80.4 us (1.17)
  the two profiles are of different devices: /device:TPU:0 before, /device:TPU:16 now
where the time goes in v3:
time: 80.4 us; the launch traced here: 80.2 us
  Pallas kernels  75.9 us (94%)
  local copies, waits for them, and re-layouts  4.26 us (5%)
    pallas_call x1, Pallas kernels, per_device(): pl.pallas_call(functools.partial(kernel, lay, experts), out_shape=jax.Sha...  75.9 us
    unnamed x3, local copies, waits for them, and re-layouts  4.26 us

profile of v3, /device:TPU:16, one launch (start us, length us, event | category | flops | bytes accessed | tf_op | source)
XLA Modules:
  0.0 80.2 jit_solution(870694373162668311)
XLA Ops:
  0.0 1.4 %copy.10.ids_in = s32[16,8]{1,0:T(8,128)} copy(s32[16,8]{0,1:T(8,128)} %param.10) | data formatting | bytes 1024 | tf_op args[1]
  1.4 1.4 %copy.11.rw_in = f32[16,8]{1,0:T(8,128)} copy(f32[16,8]{0,1:T(8,128)} %param.11) | data formatting | bytes 1024 | tf_op args[2]
  2.7 75.9 %shard_map.91 = bf16[16,3584]{1,0:T(8,128)(2,1)} custom-call(bf16[16,3584]{1,0:T(8,128)(2,1)} %tok_in.1, s32[16,8]{1,0:T(8,128)} %copy.10.ids_in, f32[16,8]{1,0:T(8,128)} %copy.11.rw_in, bf16[1,3584,512]{2,1,0:T(8,128)(2,1)} %wg_in.1, bf16[1,3584,512]{2,1,0:T(8,128)(2,1)} %wu_in.1, bf16[1,512,3584]{2,1,0:T(8,128)(2,1)} %wd_in.1, bf16[3584,512]{1,0:T(8,128)(2,1)} %sg_in.1, ...), custom_call_target="tpu_custom_call" | custom-call | tf_op jit(solution)/shard_map/pallas_call | solution.py:470
  78.6 1.6 %copy.13 = bf16[16,3584]{1,0:T(8,128)(2,1)} copy(bf16[16,3584]{1,0:T(8,128)(2,1)} %shard_map.91) | data formatting | bytes 229376

commit v4 on v3

--- a/solution.py
+++ b/solution.py
@@ -51,8 +51,8 @@
         return near, far
 
 
-def kernel(lay, experts, tok_in, ids_in, rw_in, wg_in, wu_in, wd_in, sg_in, su_in, sd_in, out,
-           tok, part, ids, rw, recvp, recvb0, recvb1, recva0, recva1, recvz0, recvz1, xs, hid, hs,
+def kernel(lay, experts, tok_in, ids, rw, wg_in, wu_in, wd_in, sg_in, su_in, sd_in, out,
+           tok, part, recvp, recvb0, recvb1, recva0, recva1, recvz0, recvz1, xs, hid, hs,
            wg, wu, wd, sg, su, sd, load_sem, tok_send, tok_recv, red_send, red_recv):
     nz, ny, nt = lay.nz, lay.ny, lay.n_tensor
     rows, half = lay.rows, lay.half
@@ -66,7 +66,6 @@
     partner = {"expert": e_idx, "tensor": t, "pair": 1 - p}
     t_peers = [(t + d) % nt for d in range(1, nt)]
     y_peers = [(y + d) % ny for d in range(1, ny)]
-    z_peers = [(z + d) % nz for d in range(1, nz)]
 
     def place(q, z_, y_, t_):
         return ((q * nz + z_) * ny + y_) * nt + t_
@@ -83,9 +82,6 @@
     own = place(p, z, y, t)
     first = pltpu.make_async_copy(tok_in, tok.at[own, :, pl.ds(0, width)], load_sem.at[6])
     first.start()
-    small = [pltpu.make_async_copy(ids_in, ids, load_sem.at[7]), pltpu.make_async_copy(rw_in, rw, load_sem.at[8])]
-    for load in small:
-        load.start()
     loads = [
         pltpu.make_async_copy(src, dst, load_sem.at[i])
         for i, (src, dst) in enumerate(
@@ -105,11 +101,15 @@
         greet(device(z, y, t_))
     for y_ in y_peers:
         greet(device(z, y_, t))
-    for z_ in z_peers:
-        greet(device(z_, y, t))
-
-    for load in small:
-        load.wait()
+
+    @pl.when(z < nz - 1)
+    def _():
+        greet(device(z + 1, y, t))
+
+    @pl.when(z > 0)
+    def _():
+        greet(device(z - 1, y, t))
+
     lane = lax.broadcasted_iota(jnp.int32, (rows, tok.shape[-1] - width), 1)
     top = ids.shape[1]
     pieces = [jnp.zeros(lane.shape, F32) for _ in range(3)]
@@ -122,7 +122,7 @@
     low = [v - h for v, h in zip(rest, mid)]
     tok[own, :, pl.ds(width, lane.shape[1])] = (hi[0] + mid[1] + low[2]).astype(BF16)
 
-    pl.semaphore_wait(barrier, nt + ny + nz - 2)
+    pl.semaphore_wait(barrier, nt + ny - 1 + jnp.minimum(z, 1) + jnp.minimum(nz - 1 - z, 1))
 
     first.wait()
 
@@ -146,9 +146,9 @@
 
     counter = [0]
 
-    def send_block(h, idx, dev):
+    def send_block(h, idx, dev, cond=None):
         view = tok.at[idx, :, wide[h]]
-        send(view, view, tok_send.at[counter[0]], tok_recv.at[h, idx], dev)
+        send(view, view, tok_send.at[counter[0]], tok_recv.at[h, idx], dev, cond)
         counter[0] += 1
 
     def arrive(h, idx):
@@ -165,8 +165,13 @@
         send_block(h, idx, partner)
 
     def line_sends(h, idx):
-        for z_ in near[1:] + far:
-            send_block(h, idx, device(z_, y, t))
+        send_block(h, idx, device(z + 1, y, t), z < nz - 1)
+        send_block(h, idx, device(z - 1, y, t), z > 0)
+
+    def onward(h, idx, z_):
+        way = 2 * jnp.minimum(jnp.maximum(z - z_, 0), 1) - 1
+        to = z + way
+        send_block(h, idx, device(to, y, t), jnp.logical_and(to >= 0, to < nz))
 
     for h in range(2):
         for f in first_peers[h]:
@@ -190,6 +195,7 @@
                 if d < len(firsts):
                     blk = place(p, z_, *yt(h, firsts[d], last_at[h]))
                     arrive(h, blk)
+                    onward(h, blk, z_)
                     last_sends(h, blk, first_at[h])
 
     def stage_last(z_):
@@ -320,9 +326,9 @@
     def buf_a(h, d):
         return recva[h].at[d], at("a", h, lay.first[h] - 1) + d
 
-    def buf_z(h, d, f):
+    def buf_z(h, slot, f):
         n = lay.first[h]
-        return recvz[h].at[d * n + f], at("z", h, (nz - 1) * n) + d * n + f
+        return recvz[h].at[slot * n + f], at("z", h, (nz + 1) * n) + slot * n + f
 
     def add_into(h, idx, others):
         v = part[idx, :, cols2[h]].astype(F32)
@@ -359,22 +365,39 @@
         return place(p, z_, y_, t_), refs
 
     def sums_line(z_):
+        gt = jnp.minimum(jnp.maximum(z_ - z, 0), 1)
+        way, slot = 2 * gt - 1, z_ + gt
+        back = z - way
+        inner = jnp.logical_and(back >= 0, back < nz)
         for f in range(max(ny, nt) - 1, -1, -1):
             for h in range(2):
                 firsts = first_peers[h] + [first_at[h]]
                 if f >= len(firsts):
                     continue
                 idx, refs = collect_last(h, z_, firsts[f])
-                add_into(h, idx, refs)
-                ref, sem = buf_z(h, (z_ - z + nz) % nz - 1, firsts[f])
-                send_sum(part.at[idx, :, cols2[h]], ref, sem, device(z_, y, t))
+                ref, sem = buf_z(h, slot, firsts[f])
+                got(ref, sem, inner)
+                chain_add(h, idx, refs, ref, inner)
+                send_sum(part.at[idx, :, cols2[h]], ref, sem, device(z + way, y, t))
+
+    def chain_add(h, idx, refs, ref, inner):
+        @pl.when(inner)
+        def _():
+            add_into(h, idx, refs + [ref])
+
+        @pl.when(jnp.logical_not(inner))
+        def _():
+            add_into(h, idx, refs)
 
     def collect_line(h, f):
         idx, refs = collect_last(h, z, f)
-        for d in range(nz - 1):
-            ref, sem = buf_z(h, d, f)
-            got(ref, sem)
-            refs.append(ref)
+        for slot, cond in ((z + 1, z > 0), (z, z < nz - 1)):
+            ref, sem = buf_z(h, slot, f)
+            got(ref, sem, cond)
+
+            @pl.when(cond)
+            def _(ref=ref):
+                add_into(h, idx, [ref])
         return idx, refs
 
     for i in range(3, 6):
@@ -404,7 +427,7 @@
     else:
         for z_ in near[::-1]:
             sums_last(z_)
-    for z_ in near[:0:-1] + far[::-1]:
+    for z_ in far[::-1] + near[:0:-1]:
         sums_line(z_)
     for h in range(2):
         for d, f in enumerate(first_peers[h]):
@@ -437,14 +460,12 @@
     halves = (cut, width - cut)
     many_b = [max(1, (lay.last[h] - 1) * nz * lay.first[h]) for h in range(2)]
     many_a = [max(1, lay.first[h] - 1) for h in range(2)]
-    many_z = [max(1, (nz - 1) * lay.first[h]) for h in range(2)]
+    many_z = [(nz + 1) * lay.first[h] for h in range(2)]
     vmem = pl.BlockSpec(memory_space=pltpu.VMEM)
     anyw = pl.BlockSpec(memory_space=pl.ANY)
     scratch = [
         pltpu.VMEM((lay.blocks, rows, width + lanes_for(experts)), BF16),
         pltpu.VMEM((lay.blocks, rows, width), BF16),
-        pltpu.VMEM(ids.shape, jnp.int32),
-        pltpu.VMEM(rw.shape, F32),
         pltpu.VMEM((lay.half, rows, width), BF16),
         pltpu.VMEM((many_b[0], rows, halves[0]), BF16),
         pltpu.VMEM((many_b[1], rows, halves[1]), BF16),
@@ -470,7 +491,7 @@
     return pl.pallas_call(
         functools.partial(kernel, lay, experts),
         out_shape=jax.ShapeDtypeStruct((rows, width), BF16),
-        in_specs=[anyw] * 9,
+        in_specs=[anyw, vmem, vmem] + [anyw] * 6,
         out_specs=vmem,
         scratch_shapes=scratch,
         compiler_params=pltpu.CompilerParams(

time: 80.4 us -> 76.5 us (0.951)
  the two profiles are of different devices: /device:TPU:16 before, /device:TPU:0 now
where the time goes in v4:
time: 76.5 us; the launch traced here: 76.2 us
  Pallas kernels  71.9 us (94%)
  local copies, waits for them, and re-layouts  4.26 us (6%)
    pallas_call x1, Pallas kernels, per_device(): pl.pallas_call(functools.partial(kernel, lay, experts), out_shape=jax.Sha...  71.9 us
    unnamed x3, local copies, waits for them, and re-layouts  4.26 us

profile of v4, /device:TPU:0, one launch (start us, length us, event | category | flops | bytes accessed | tf_op | source)
XLA Modules:
  0.0 76.2 jit_solution(7442447930606087520)
XLA Ops:
  0.0 1.4 %copy.10.ids = s32[16,8]{1,0:T(8,128)} copy(s32[16,8]{0,1:T(8,128)} %param.10) | data formatting | bytes 1024 | tf_op args[1]
  1.4 1.4 %copy.11.rw = f32[16,8]{1,0:T(8,128)} copy(f32[16,8]{0,1:T(8,128)} %param.11) | data formatting | bytes 1024 | tf_op args[2]
  2.7 71.9 %shard_map.91 = bf16[16,3584]{1,0:T(8,128)(2,1)} custom-call(bf16[16,3584]{1,0:T(8,128)(2,1)} %tok_in.1, s32[16,8]{1,0:T(8,128)} %copy.10.ids, f32[16,8]{1,0:T(8,128)} %copy.11.rw, bf16[1,3584,512]{2,1,0:T(8,128)(2,1)} %wg_in.1, bf16[1,3584,512]{2,1,0:T(8,128)(2,1)} %wu_in.1, bf16[1,512,3584]{2,1,0:T(8,128)(2,1)} %wd_in.1, bf16[3584,512]{1,0:T(8,128)(2,1)} %sg_in.1, ...), custom_call_target="tpu_custom_call" | custom-call | tf_op jit(solution)/shard_map/pallas_call | solution.py:491
  74.7 1.6 %copy.13 = bf16[16,3584]{1,0:T(8,128)(2,1)} copy(bf16[16,3584]{1,0:T(8,128)(2,1)} %shard_map.91) | data formatting | bytes 229376
